TPU v7x, 32 devices: a whole 2x2x4 slice. The times are simulated.
32 devices in a mesh: store: 8 (over z, y), tensor: 4 (over x, core).
Axes of the slice: x: 2, y: 2, z: 4, core: 2. Of those that a mesh axis runs over, the one named last changes fastest.
Arguments:
- tokens: bfloat16 [8192, 8192], P('store', 'tensor'), may hold values from -1200 to 1200
- norm_gain: float32 [8192], P('tensor'), may hold values from 0.1 to 1.9
- kv_weight: bfloat16 [8192, 2, 1024], P('tensor'), may hold values from -0.0625 to 0.0625
- adapter_down: bfloat16 [32, 8192, 128], P('store', 'tensor'), may hold values from -0.0625 to 0.0625
- adapter_up: bfloat16 [32, 2, 64, 1024], P('store', None, None, 'tensor'), may hold values from -0.75 to 0.75
- token_adapters: int32 [8192, 1], P('store'), may hold values from 0 to 31; in each aligned block of 1024 rows (0 to 1023, 1024 to 2047, ...) at most 40 rows name the same one
- adapter_slot: int32 [32], replicated, may hold values from 0 to 31, each once
- request_lengths: int32 [16], replicated, may hold values from 1 to 4096, 8192 in all
Outputs:
- new_keys: bfloat16 [8192, 1024], P('store', 'tensor')
- new_values: bfloat16 [8192, 1024], P('store', 'tensor')
Inputs may be any that keep to these rules, and one draw needn't show every extreme that they name: `token_adapters`: among the 1024 tokens of one index of store no adapter is named more than 40 times; in every draw some adapter is named exactly 40 times by the tokens of some index. `adapter_slot`: each row 0 to 31 appears once. `request_lengths`: the lengths sum to 8192; the largest is exactly 4096.
All inputs are finite; a program needn't handle non-finite values.
Results may differ from a plain program's by a relative error of at most 0.0061.
Values may be sent and summed in bfloat16 or wider, within the bound.
A program may use at most 128 MiB of HBM per device.

v0:
```python
import math
import jax
import jax.numpy as jnp
from jax import lax
from jax.sharding import PartitionSpec as P

D = 8192
HEAD = 128
ADAPTER_RANK = 64
epsilon = 1e-05
adapter_scale = 2.0
rope_theta = 500000.0


def place_rows(adapter_ids, adapter_slot, capacity):
    catalog = jnp.arange(adapter_slot.shape[0], dtype=jnp.int32)
    slot_rows = jnp.sum(
        jnp.where(adapter_ids[:, None] == catalog[None, :], adapter_slot[None, :], 0), axis=1
    )
    row_order = jnp.arange(adapter_ids.shape[0], dtype=jnp.int32)
    same_earlier = (adapter_ids[:, None] == adapter_ids[None, :]) & (
        row_order[None, :] < row_order[:, None]
    )
    rank_rows = jnp.sum(same_earlier.astype(jnp.int32), axis=1)
    return slot_rows * capacity + rank_rows


def positions_of(first_row, row_count, lengths):
    global_rows = first_row + jnp.arange(row_count, dtype=jnp.int32)
    request_ends = jnp.cumsum(lengths)
    preceding = jnp.sum(
        jnp.where(request_ends[None, :] <= global_rows[:, None], lengths[None, :], 0), axis=1
    )
    return global_rows - preceding


def rotate(states, positions):
    per_head = states.reshape(states.shape[0], -1, HEAD)
    half_size = HEAD // 2
    frequency = jnp.exp(
        jnp.arange(half_size, dtype=jnp.float32) * (-2.0 * math.log(rope_theta) / HEAD)
    )
    angles = positions.astype(jnp.float32)[:, None] * frequency[None, :]
    cos_part = jnp.concatenate([jnp.cos(angles), jnp.cos(angles)], axis=1)[:, None, :]
    sin_part = jnp.concatenate([jnp.sin(angles), jnp.sin(angles)], axis=1)[:, None, :]
    low_half = per_head[..., :half_size]
    high_half = per_head[..., half_size:]
    turned = jnp.concatenate([-high_half, low_half], axis=-1)
    return (per_head * cos_part + turned * sin_part).reshape(states.shape)


def local(
    tokens,
    norm_gain,
    kv_weight,
    adapter_down,
    adapter_up,
    token_adapters,
    adapter_slot,
    request_lengths,
):
    row_count = tokens.shape[0]
    local_width = tokens.shape[1]
    adapter_total = adapter_slot.shape[0]
    capacity = max(2, 5 * row_count // (4 * adapter_total))
    store_size = lax.axis_size("store")
    per_owner = adapter_down.shape[0]
    kv_local = adapter_up.shape[3]
    widened = tokens.astype(jnp.float32)
    squares = lax.psum(jnp.sum(widened * widened, axis=1), "tensor")
    normed = (widened * lax.rsqrt(squares / D + epsilon)[:, None] * norm_gain[None, :]).astype(
        jnp.bfloat16
    )
    targets = place_rows(token_adapters[:, 0], adapter_slot, capacity)
    send_rows = (
        jnp.zeros((adapter_total * capacity, local_width), jnp.bfloat16).at[targets].set(normed)
    )
    send_rows = send_rows.reshape(store_size, per_owner, capacity, local_width)
    down_projected = jnp.einsum(
        "slcd,ldr->slcr",
        lax.all_to_all(send_rows, "store", split_axis=0, concat_axis=0, tiled=True),
        adapter_down,
        preferred_element_type=jnp.float32,
    )
    rank_total_sum = lax.psum(down_projected, "tensor")
    rank_activation = (rank_total_sum * adapter_scale).astype(jnp.bfloat16)
    split_rank = rank_activation.reshape(rank_activation.shape[:3] + (2, ADAPTER_RANK))
    update_rows = jnp.einsum(
        "slcjr,ljrk->slcjk", split_rank, adapter_up, preferred_element_type=jnp.float32
    )
    back_rows = update_rows.astype(jnp.bfloat16).reshape(
        rank_activation.shape[:3] + (2 * kv_local,)
    )
    returned = lax.all_to_all(back_rows, "store", split_axis=0, concat_axis=0, tiled=True)
    delta_rows = returned.reshape(adapter_total * capacity, 2, kv_local)[targets]
    partial_value = jnp.einsum("td,djk->tjk", normed, kv_weight, preferred_element_type=jnp.float32)
    base_part = lax.psum_scatter(partial_value, "tensor", scatter_dimension=2, tiled=True)
    combined = base_part + delta_rows.astype(jnp.float32)
    positions = positions_of(lax.axis_index("store") * row_count, row_count, request_lengths)
    new_keys = rotate(combined[:, 0, :], positions).astype(jnp.bfloat16)
    new_values = combined[:, 1, :].astype(jnp.bfloat16)
    return (new_keys, new_values)


def solution(mesh):
    return jax.shard_map(
        local,
        mesh=mesh,
        in_specs=(
            P("store", "tensor"),
            P("tensor"),
            P("tensor", None, None),
            P("store", "tensor", None),
            P("store", None, None, "tensor"),
            P("store", None),
            P(),
            P(),
        ),
        out_specs=(P("store", "tensor"), P("store", "tensor")),
        check_vma=False,
    )
```

profile of v0, /device:TPU:0, one launch (start us, length us, event | category | flops | bytes accessed | tf_op | source)
XLA Modules:
  0.0 278.7 jit_solution(12801032871038219586)
XLA Ops:
  7.2 1.4 convert_reduce_fusion
  9.4 3.1 %fusion = f32[1024]{0:T(1024)S(1)} fusion(bf16[1024,2048]{1,0:T(8,128)(2,1)} %param.8), kind=kLoop, calls=%fused_computation.4 | loop fusion | flops 6290432 | bytes 4198400 | tf_op jit(solution)/shard_map/reduce_sum | solution.py:70
  12.5 8.4 %psum.14 = f32[1024]{0:T(1024)S(1)} all-reduce(f32[1024]{0:T(1024)S(1)} %fusion), channel_id=1, replica_groups=mesh['store'=8,'tensor'=4] {'tensor'}, use_global_device_ids=true, to_apply=%region_1.0 | all-reduce | flops 1024 | bytes 8192 | tf_op jit(solution)/shard_map/psum | solution.py:70
  20.9 11.2 %scatter_custom_fusion = bf16[1280,2048]{1,0:T(8,128)(2,1)} fusion(s32[1024]{0:T(1024)S(1)} %bitcast.50, bf16[]{:T(256)} %constant.6.clone.1, bf16[1024,2048]{1,0:T(8,128)(2,1)} %param.8, f32[2048]{0:T(1024)S(1)} %copy-done.6, f32[1024]{0:T(1024)S(1)} %add_rsqrt_fusion), kind=kCustom, calls=%fused_computation.15 | custom fusion | flops 8388608 | bytes 9449474 | tf_op jit(solution)/shard_map/scatter | solution.py:76
  32.1 120.3 %all_to_all.10 = bf16[8,4,40,2048]{3,2,1,0:T(8,128)(2,1)S(1)} all-to-all(bf16[8,4,40,2048]{3,2,1,0:T(8,128)(2,1)} %bitcast.46), channel_id=1, replica_groups=mesh['store'=8,'tensor'=4] {'store'}, dimensions={0} | all-to-all | bytes 10485760 | tf_op jit(solution)/shard_map/all_to_all | solution.py:81
  152.4 2.5 fusion.13
  155.1 14.9 %fusion.3 = f32[1024,2,1024]{2,0,1:T(8,128)} fusion(bf16[2048,2,1024]{2,1,0:T(2,128)(2,1)} %param.10, bf16[1024,2048]{1,0:T(8,128)(2,1)} %param.8, f32[2048]{0:T(1024)S(1)} %copy-done.6, f32[1024]{0:T(1024)S(1)} %add_rsqrt_fusion), kind=kOutput, calls=%fused_computation.7 | convolution fusion | flops 8598323200 | bytes 20983808 | tf_op jit(solution)/shard_map/td,djk->tjk/dot_general | solution.py:96
  170.0 18.1 %all-reduce.2.cloned.1.call-done = f32[8,4,40,128]{3,2,0,1:T(8,128)} async-done(((f32[8,4,40,128]{3,2,0,1:T(8,128)}), f32[8,4,40,128]{3,2,0,1:T(8,128)}) %all-reduce.2.cloned.1.call-update) | async-done | bytes 655376 | tf_op jit(solution)/shard_map/psum | solution.py:85
  188.1 1.1 multiply_convert_fusion
  190.1 1.3 copy.28
  191.5 1.7 reshape.97
  193.2 5.5 %all-to-all-start.1 = ((bf16[8,4,40,512]{3,2,1,0:T(8,128)(2,1)}), bf16[8,4,40,512]{3,2,1,0:T(8,128)(2,1)S(1)}, u32[]{:S(2)}, u32[]{:S(2)}) async-start(bf16[8,4,40,512]{3,2,1,0:T(8,128)(2,1)} %reshape.97), calls=%async_computation.2 | async-start | bytes 2621440 | tf_op jit(solution)/shard_map/all_to_all | solution.py:94
  199.0 1.9 multiply_cosine_fusion
  200.9 1.3 pad_maximum_fusion
  202.2 27.2 %all-to-all-done.1 = bf16[8,4,40,512]{3,2,1,0:T(8,128)(2,1)S(1)} async-done(((bf16[8,4,40,512]{3,2,1,0:T(8,128)(2,1)}), bf16[8,4,40,512]{3,2,1,0:T(8,128)(2,1)S(1)}, u32[]{:S(2)}, u32[]{:S(2)}) %all-to-all-start.1) | async-done | bytes 1310752 | tf_op jit(solution)/shard_map/all_to_all | solution.py:94
  229.4 1.2 reshape.98
  230.6 5.5 %gather_fusion = bf16[1024,2,256]{2,1,0:T(2,128)(2,1)S(1)} fusion(bf16[1280,2,256]{2,1,0:T(2,128)(2,1)} %reshape.98, s32[1024]{0:T(1024)S(1)} %broadcast_clamp_fusion), kind=kCustom, calls=%fused_computation | custom fusion | bytes 2101248 | tf_op jit(solution)/shard_map/gather | solution.py:95
  236.1 25.9 %reduce-scatter.2.cloned.1.call-done = f32[1024,2,256]{2,0,1:T(8,128)} async-done(((f32[1024,2,1024]{2,0,1:T(8,128)}), f32[1024,2,256]{2,0,1:T(8,128)}) %reduce-scatter.2.cloned.1.call-update) | async-done | bytes 2097168 | tf_op jit(solution)/shard_map/reduce_scatter | solution.py:97
  262.0 1.8 convert_add_fusion
  263.8 1.1 slice.19
  266.3 1.7 reshape_squeeze.6
  268.1 1.1 slice_negate_fusion
  269.3 1.2 maximum_multiply_fusion
  270.9 1.0 fusion.20
  (36 shorter events, 4.0 us)
Async XLA Ops:
  7.2 145.2 %copy-start = (bf16[4,2048,128]{2,1,0:T(8,128)(2,1)S(1)}, bf16[4,2048,128]{2,1,0:T(8,128)(2,1)}, u32[]{:S(2)}) copy-start(bf16[4,2048,128]{2,1,0:T(8,128)(2,1)} %param.11) | copy-start | bytes 6291460
  7.2 13.7 %copy-start.6 = (f32[2048]{0:T(1024)S(1)}, f32[2048]{0:T(1024)}, u32[]{:S(2)}) copy-start(f32[2048]{0:T(1024)} %param.9) | copy-start | bytes 24580
  7.2 180.9 %all-reduce.2.cloned.1.call-start = ((), (), s32[]{:S(2)}) async-start(), calls=%async_computation.4 | async-start | bytes 1310720 | tf_op jit(solution)/shard_map/psum | solution.py:85
  154.9 107.1 %reduce-scatter.2.cloned.1.call-start = ((), (), s32[]{:S(2)}) async-start(), calls=%async_computation.3 | async-start | bytes 10485760 | tf_op jit(solution)/shard_map/reduce_scatter | solution.py:97
  170.0 19.6 %copy-start.5 = (bf16[4,2,64,256]{3,2,1,0:T(8,128)(2,1)S(1)}, bf16[4,2,64,256]{3,2,1,0:T(8,128)(2,1)}, u32[]{:S(2)}) copy-start(bf16[4,2,64,256]{3,2,1,0:T(8,128)(2,1)} %param.12) | copy-start | bytes 786436
  190.1 8.6 %copy-start.7 = (s32[16]{0:T(128)S(1)}, s32[16]{0:T(128)}, u32[]{:S(2)}) copy-start(s32[16]{0:T(128)} %param.15) | copy-start | bytes 196
  193.2 36.3 %all-to-all-start.1 = ((bf16[8,4,40,512]{3,2,1,0:T(8,128)(2,1)}), bf16[8,4,40,512]{3,2,1,0:T(8,128)(2,1)S(1)}, u32[]{:S(2)}, u32[]{:S(2)}) async-start(bf16[8,4,40,512]{3,2,1,0:T(8,128)(2,1)} %reshape.97), calls=%async_computation.2 | async-start | bytes 2621440 | tf_op jit(solution)/shard_map/all_to_all | solution.py:94
  263.8 1.7 copy-start.1
  268.1 1.2 copy-start.4
  268.1 2.4 copy-start.3
  268.1 2.8 copy-start.2
Sparse Core Ops, SparseCore 0:
  155.0 33.0 all-reduce.1
  190.7 71.2 reduce-scatter.1
where the time goes:
time: 279 us
  blocking collectives  129 us (46%)
  waiting for transfers between devices  71.1 us (25%)
  other arithmetic  26.2 us (9%)
  matrix products  17.9 us (6%)
  local copies, waits for them, and re-layouts  14.8 us (5%)
  between operations  14.2 us (5%)
  starting transfers between devices  5.78 us (2%)
    all_to_all x1, blocking collectives, local(): lax.all_to_all(send_rows, 'store', split_axis=0, concat_axis=0, tiled=True)  120 us
    all_to_all x1, waiting for transfers between devices, local(): lax.all_to_all(back_rows, 'store', split_axis=0, concat_axis=0, tiled=True)  27.2 us
    reduce_scatter x1, waiting for transfers between devices, local(): lax.psum_scatter(partial_value, 'tensor', scatter_dimension=2, tiled=True)  25.9 us
    psum x1, waiting for transfers between devices, local(): rank_total_sum = lax.psum(down_projected, 'tensor')  18.1 us
    dot_general x1, matrix products, local(): jnp.einsum('td,djk->tjk', normed, kv_weight, preferred_element_type=jnp.f...  14.9 us
    scatter x1, other arithmetic, local(): jnp.zeros((adapter_total * capacity, local_width), jnp.bfloat16).at[targets]  11.2 us
    psum x1, blocking collectives, local(): squares = lax.psum(jnp.sum(widened * widened, axis=1), 'tensor')  8.38 us
  transfers between devices with their start and end apart: 3, of which 3 were waited for; matrix products, arithmetic and copies ran while one was open for 11% of the time, Pallas kernels for 0%

commit v1 on v0

--- a/solution.py
+++ b/solution.py
@@ -10,6 +10,14 @@
 epsilon = 1e-05
 adapter_scale = 2.0
 rope_theta = 500000.0
+
+
+def doubling_sum(x, mesh_axis):
+    size, total = (lax.axis_size(mesh_axis), x)
+    for hop in [1 << k for k in range(size.bit_length() - 1)]:
+        swap = [(i, i ^ hop) for i in range(size)]
+        total = total + lax.ppermute(total, mesh_axis, swap)
+    return total
 
 
 def place_rows(adapter_ids, adapter_slot, capacity):
@@ -82,7 +90,7 @@
         adapter_down,
         preferred_element_type=jnp.float32,
     )
-    rank_total_sum = lax.psum(down_projected, "tensor")
+    rank_total_sum = doubling_sum(down_projected, "tensor")
     rank_activation = (rank_total_sum * adapter_scale).astype(jnp.bfloat16)
     split_rank = rank_activation.reshape(rank_activation.shape[:3] + (2, ADAPTER_RANK))
     update_rows = jnp.einsum(

time: 279 us -> 251 us (0.90)
  waiting for transfers between devices: 71.1 us -> 44.8 us
    reduce_scatter x1, waiting for transfers between devices: 25.9 us -> 0.02 us  [local(): lax.psum_scatter(partial_value, 'tensor', scatter_dimension=2, tiled=True)]
    psum x1 -> x0, waiting for transfers between devices: 18.1 us -> none  [local(): rank_total_sum = lax.psum(down_projected, 'tensor')]
    ppermute x0 -> x2, waiting for transfers between devices: none -> 17.3 us  [doubling_sum(): total = total + lax.ppermute(total, mesh_axis, swap)]
  transfers between devices with their start and end apart: 3 -> 4, of which waited for: 3 -> 3; matrix products, arithmetic and copies ran while one was open for 11% -> 12% of each run, Pallas kernels for 0% -> 0%
where the time goes in v1:
time: 251 us
  blocking collectives  129 us (51%)
  waiting for transfers between devices  44.8 us (18%)
  other arithmetic  24.9 us (10%)
  matrix products  17 us (7%)
  local copies, waits for them, and re-layouts  15.6 us (6%)
  between operations  14.3 us (6%)
  starting transfers between devices  5.32 us (2%)
    all_to_all x1, blocking collectives, local(): lax.all_to_all(send_rows, 'store', split_axis=0, concat_axis=0, tiled=True)  120 us
    all_to_all x1, waiting for transfers between devices, local(): lax.all_to_all(back_rows, 'store', split_axis=0, concat_axis=0, tiled=True)  27.4 us
    ppermute x2, waiting for transfers between devices, doubling_sum(): total = total + lax.ppermute(total, mesh_axis, swap)  17.3 us
    dot_general x1, matrix products, local(): jnp.einsum('td,djk->tjk', normed, kv_weight, preferred_element_type=jnp.f...  14.9 us
    scatter x1, other arithmetic, local(): jnp.zeros((adapter_total * capacity, local_width), jnp.bfloat16).at[targets]  12.2 us
    psum x1, blocking collectives, local(): squares = lax.psum(jnp.sum(widened * widened, axis=1), 'tensor')  8.38 us
    gather x1, local copies, waits for them, and re-layouts, local(): returned.reshape(adapter_total * capacity, 2, kv_local)[targets]  5.5 us
  transfers between devices with their start and end apart: 4, of which 3 were waited for; matrix products, arithmetic and copies ran while one was open for 12% of the time, Pallas kernels for 0%

profile of v1, /device:TPU:0, one launch (start us, length us, event | category | flops | bytes accessed | tf_op | source)
XLA Modules:
  0.0 250.5 jit_solution(16292247925499808871)
XLA Ops:
  7.2 3.2 %fusion = f32[1024]{0:T(1024)S(1)} fusion(bf16[1024,2048]{1,0:T(8,128)(2,1)} %param.8), kind=kLoop, calls=%fused_computation.4 | loop fusion | flops 6290432 | bytes 4198400 | tf_op jit(solution)/shard_map/reduce_sum | solution.py:78
  10.4 8.4 %psum.7 = f32[1024]{0:T(1024)S(1)} all-reduce(f32[1024]{0:T(1024)S(1)} %fusion), channel_id=1, replica_groups=mesh['store'=8,'tensor'=4] {'tensor'}, use_global_device_ids=true, to_apply=%region_1.0 | all-reduce | flops 1024 | bytes 8192 | tf_op jit(solution)/shard_map/psum | solution.py:78
  18.8 14.9 %fusion.3 = f32[1024,2,1024]{2,0,1:T(8,128)} fusion(bf16[2048,2,1024]{2,1,0:T(2,128)(2,1)} %param.10, bf16[1024,2048]{1,0:T(8,128)(2,1)} %param.8, f32[2048]{0:T(1024)S(1)} %copy-done.6, f32[1024]{0:T(1024)S(1)} %add_rsqrt_fusion), kind=kOutput, calls=%fused_computation.7 | convolution fusion | flops 8598323200 | bytes 20983808 | tf_op jit(solution)/shard_map/td,djk->tjk/dot_general | solution.py:104
  35.0 12.2 %scatter_custom_fusion = bf16[1280,2048]{1,0:T(8,128)(2,1)} fusion(s32[1024]{0:T(1024)S(1)} %bitcast.50, bf16[]{:T(256)} %constant.6.clone.1, bf16[1024,2048]{1,0:T(8,128)(2,1)} %param.8, f32[2048]{0:T(1024)S(1)} %copy-done.6, f32[1024]{0:T(1024)S(1)} %add_rsqrt_fusion), kind=kCustom, calls=%fused_computation.15 | custom fusion | flops 8388608 | bytes 9449474 | tf_op jit(solution)/shard_map/scatter | solution.py:84
  47.3 120.3 %all_to_all.10 = bf16[8,4,40,2048]{3,2,1,0:T(8,128)(2,1)S(1)} all-to-all(bf16[8,4,40,2048]{3,2,1,0:T(8,128)(2,1)} %bitcast.46), channel_id=1, replica_groups=mesh['store'=8,'tensor'=4] {'store'}, dimensions={0} | all-to-all | bytes 10485760 | tf_op jit(solution)/shard_map/all_to_all | solution.py:89
  167.5 1.7 fusion.13
  169.3 2.1 collective-permute-done
  171.5 1.6 collective-permute-start.1
  173.1 15.2 %collective-permute-done.1 = f32[8,4,40,128]{3,2,0,1:T(8,128)S(1)} collective-permute-done((f32[8,4,40,128]{3,2,0,1:T(8,128)S(1)}, f32[8,4,40,128]{3,2,0,1:T(8,128)S(1)}, u32[]{:S(2)}, u32[]{:S(2)}) %collective-permute-start.1) | collective-permute-done | bytes 655392 | tf_op jit(solution)/shard_map/ppermute | solution.py:19
  189.2 1.3 copy.28
  190.6 1.7 reshape.97
  192.3 3.6 %all-to-all-start.1 = ((bf16[8,4,40,512]{3,2,1,0:T(8,128)(2,1)}), bf16[8,4,40,512]{3,2,1,0:T(8,128)(2,1)S(1)}, u32[]{:S(2)}, u32[]{:S(2)}) async-start(bf16[8,4,40,512]{3,2,1,0:T(8,128)(2,1)} %reshape.97), calls=%async_computation.2 | async-start | bytes 2621440 | tf_op jit(solution)/shard_map/all_to_all | solution.py:102
  196.3 1.9 multiply_cosine_fusion
  198.2 1.3 pad_maximum_fusion
  199.5 27.4 %all-to-all-done.1 = bf16[8,4,40,512]{3,2,1,0:T(8,128)(2,1)S(1)} async-done(((bf16[8,4,40,512]{3,2,1,0:T(8,128)(2,1)}), bf16[8,4,40,512]{3,2,1,0:T(8,128)(2,1)S(1)}, u32[]{:S(2)}, u32[]{:S(2)}) %all-to-all-start.1) | async-done | bytes 1310752 | tf_op jit(solution)/shard_map/all_to_all | solution.py:102
  226.9 1.3 reshape.98
  228.2 5.5 %gather_fusion = bf16[1024,2,256]{2,1,0:T(2,128)(2,1)S(1)} fusion(bf16[1280,2,256]{2,1,0:T(2,128)(2,1)} %reshape.98, s32[1024]{0:T(1024)S(1)} %broadcast_clamp_fusion), kind=kCustom, calls=%fused_computation | custom fusion | bytes 2101248 | tf_op jit(solution)/shard_map/gather | solution.py:103
  233.8 1.8 convert_add_fusion
  235.6 1.1 slice.19
  237.2 0.8 fusion.22
  238.1 1.7 reshape_squeeze.6
  239.9 1.1 slice_negate_fusion
  241.0 1.2 maximum_multiply_fusion
  242.6 1.0 fusion.20
  (42 shorter events, 3.7 us)
Async XLA Ops:
  7.2 160.4 %copy-start = (bf16[4,2048,128]{2,1,0:T(8,128)(2,1)S(1)}, bf16[4,2048,128]{2,1,0:T(8,128)(2,1)}, u32[]{:S(2)}) copy-start(bf16[4,2048,128]{2,1,0:T(8,128)(2,1)} %param.11) | copy-start | bytes 6291460
  7.2 11.7 %copy-start.6 = (f32[2048]{0:T(1024)S(1)}, f32[2048]{0:T(1024)}, u32[]{:S(2)}) copy-start(f32[2048]{0:T(1024)} %param.9) | copy-start | bytes 24580
  7.2 226.6 %reduce-scatter.2.cloned.1.call-start = ((), (), s32[]{:S(2)}) async-start(), calls=%async_computation.3 | async-start | bytes 10485760 | tf_op jit(solution)/shard_map/reduce_scatter | solution.py:105
  33.7 0.7 copy-start.7
  33.7 0.7 copy-start.9
  169.2 19.5 %copy-start.5 = (bf16[4,2,64,256]{3,2,1,0:T(8,128)(2,1)S(1)}, bf16[4,2,64,256]{3,2,1,0:T(8,128)(2,1)}, u32[]{:S(2)}) copy-start(bf16[4,2,64,256]{3,2,1,0:T(8,128)(2,1)} %param.12) | copy-start | bytes 786436
  169.2 2.2 collective-permute-start
  171.5 16.8 %collective-permute-start.1 = (f32[8,4,40,128]{3,2,0,1:T(8,128)S(1)}, f32[8,4,40,128]{3,2,0,1:T(8,128)S(1)}, u32[]{:S(2)}, u32[]{:S(2)}) collective-permute-start(f32[8,4,40,128]{3,2,0,1:T(8,128)S(1)} %add.65), channel_id=1, source_target_pairs={{0,2},{1,3},{2,0},{3,1},{4,6},{5,7},{6,4},{7,5},{8,10},{9,11},{10,... | collective-permute-start | bytes 1966088 | tf_op jit(solution)/shard_map/ppermute | solution.py:19
  189.2 6.7 %copy-start.8 = (s32[16]{0:T(128)S(1)}, s32[16]{0:T(128)}, u32[]{:S(2)}) copy-start(s32[16]{0:T(128)} %param.15) | copy-start | bytes 196
  192.3 34.6 %all-to-all-start.1 = ((bf16[8,4,40,512]{3,2,1,0:T(8,128)(2,1)}), bf16[8,4,40,512]{3,2,1,0:T(8,128)(2,1)S(1)}, u32[]{:S(2)}, u32[]{:S(2)}) async-start(bf16[8,4,40,512]{3,2,1,0:T(8,128)(2,1)} %reshape.97), calls=%async_computation.2 | async-start | bytes 2621440 | tf_op jit(solution)/shard_map/all_to_all | solution.py:102
  235.6 1.7 copy-start.1
  239.8 1.2 copy-start.4
  239.8 2.4 copy-start.3
  239.9 2.8 %copy-start.2 = (f32[1024,2,256]{2,0,1:T(8,128)S(1)}, f32[1024,2,256]{2,0,1:T(8,128)}, u32[]{:S(2)}) copy-start(f32[1024,2,256]{2,0,1:T(8,128)} %copy-done.1) | copy-start | bytes 6291460
Sparse Core Ops, SparseCore 0:
  33.9 71.5 reduce-scatter.1
